TPU v7x, 32 devices: a whole 2x2x4 slice. The times are simulated.
32 devices in a mesh: shot: 2 (over x), freq: 16 (over z, y, core).
Axes of the slice: x: 2, y: 2, z: 4, core: 2. Of those that a mesh axis runs over, the one named last changes fastest.
Arguments:
- receiver_data: float32 [64, 2, 32, 1024], P(('shot', 'freq')), parts along dimension 0, may hold values from -6 to 6
- source_spectrum: float32 [32, 2], P('freq'), may hold values from -4 to 4
- filter_taps: float32 [32, 4, 6], P('freq'), may hold values from -1.5 to 1.5, as said below
- slowness: float32 [16, 32, 1024], P('freq'), may hold values from 0.5 to 2
- depth_owner: int32 [6], P('shot'), parts along dimension 0, may hold values from 0 to 15
- source_position: int32 [4], P('shot'), parts along dimension 0, may hold values from 0 to 31
Outputs:
- migrated_image: float32 [32, 32, 1024], P(('shot', 'freq')), parts along dimension 0
There are 2 independent parts, one for each index of `shot`. A program takes and returns all parts, laid end to end along the dimension named above; an argument that names none is the same for every part. Nothing has to cross between parts.
Inputs may be any that keep to these rules, and one draw needn't show every extreme that they name: `filter_taps`: each frequency and direction holds three complex taps.
All inputs are finite; a program needn't handle non-finite values.
Results may differ from a plain program's by a relative error of at most 0.0001.
Values sent between devices are 32-bit elements; how exact they have to be, the bound alone decides.
A program may use at most 64 MiB of HBM per device.

v0:
```python
import math

import jax
import jax.numpy as jnp
from jax import lax
from jax.sharding import PartitionSpec as P

lens_rate = 3.0
wave_rate = 0.5
directions = ((1, 0), (0, 1), (1, 1), (1, -1))


def broadcast(value, axis, source):
    kept = jnp.where(lax.axis_index(axis) == source, value, 0).astype(value.dtype)
    return lax.psum(kept, axis)


def source_start(spectrum, position, freq_index, freq_total, height, breadth):
    src_row = position[0].astype(jnp.float32)
    src_col = position[1].astype(jnp.float32)
    row_axis = jnp.arange(height, dtype=jnp.float32)[:, None]
    col_axis = jnp.arange(breadth, dtype=jnp.float32)[None, :]
    distance = jnp.sqrt((row_axis - src_row) ** 2 + (col_axis - src_col) ** 2 + 1.0)
    amplitude = 1.0 / (1.0 + distance / (height / 4.0))
    wavenumber = (freq_index.astype(jnp.float32) + 1.0) * (wave_rate / freq_total)
    phase_map = wavenumber[:, None, None] * distance[None]
    base_re = amplitude[None] * jnp.cos(phase_map)
    base_im = -amplitude[None] * jnp.sin(phase_map)
    wave_re = spectrum[:, 0][:, None, None]
    wave_im = spectrum[:, 1][:, None, None]
    return jnp.stack(
        [wave_re * base_re - wave_im * base_im, wave_re * base_im + wave_im * base_re], axis=1
    )


def complex_mul(values, coef_re, coef_im):
    coef_re = coef_re[:, None, None]
    coef_im = coef_im[:, None, None]
    return jnp.stack(
        [
            values[:, 0] * coef_re - values[:, 1] * coef_im,
            values[:, 0] * coef_im + values[:, 1] * coef_re,
        ],
        axis=1,
    )


def thin_lens(wavefield, layer_slab, freq_index, freq_total, handed):
    phases = (
        (freq_index.astype(jnp.float32) + 1.0)[:, None, None]
        * (lens_rate / freq_total)
        * layer_slab[None]
    )
    rot_re = jnp.cos(phases)
    rot_im = handed * jnp.sin(phases)
    part_re = wavefield[:, 0]
    part_im = wavefield[:, 1]
    return jnp.stack(
        [part_re * rot_re - part_im * rot_im, part_re * rot_im + part_im * rot_re], axis=1
    )


def directional(wavefield, coeffs, step_x, step_y, handed):
    height = wavefield.shape[2]
    breadth = wavefield.shape[3]
    padded = jnp.pad(wavefield, ((0, 0), (0, 0), (2, 2), (2, 2)))

    def adjacent(offset):
        return padded[
            :,
            :,
            2 + offset * step_x : 2 + offset * step_x + height,
            2 + offset * step_y : 2 + offset * step_y + breadth,
        ]

    inner_pair = adjacent(1) + adjacent(-1)
    outer_pair = adjacent(2) + adjacent(-2)
    result = complex_mul(wavefield, coeffs[:, 0], handed * coeffs[:, 1])
    result = result + complex_mul(inner_pair, coeffs[:, 2], handed * coeffs[:, 3])
    return result + complex_mul(outer_pair, coeffs[:, 4], handed * coeffs[:, 5])


def depth_step(source, receiver, layer_slab, filter_taps, freq_index, freq_total):
    source = thin_lens(source, layer_slab, freq_index, freq_total, -1.0)
    receiver = thin_lens(receiver, layer_slab, freq_index, freq_total, 1.0)
    for direction, (step_x, step_y) in enumerate(directions):
        source = directional(source, filter_taps[:, direction], step_x, step_y, 1.0)
        receiver = directional(receiver, filter_taps[:, direction], step_x, step_y, -1.0)
    return (source, receiver)


def local(receiver_data, source_spectrum, filter_taps, slowness, depth_owner, source_position):
    freq_local = receiver_data.shape[0]
    height = receiver_data.shape[2]
    breadth = receiver_data.shape[3]
    device_rank = lax.axis_index("freq")
    freq_total = lax.axis_size("freq") * freq_local
    freq_index = device_rank * freq_local + jnp.arange(freq_local, dtype=jnp.int32)
    source = source_start(source_spectrum, source_position, freq_index, freq_total, height, breadth)
    receiver = receiver_data
    migrated = jnp.zeros((1, height, breadth), jnp.float32)
    partials = []
    masks = []
    for level in range(depth_owner.shape[0]):
        owner_now = depth_owner[level]
        layer_slab = broadcast(slowness[0], "freq", owner_now)
        source, receiver = depth_step(
            source, receiver, layer_slab, filter_taps, freq_index, freq_total
        )
        local_term = jnp.sum(
            source[:, 0] * receiver[:, 0] + source[:, 1] * receiver[:, 1], axis=0
        ) / math.sqrt(freq_total)
        owner_mask = (owner_now == device_rank).astype(jnp.float32)
        partials.append(local_term)
        masks.append(owner_mask)
    summed_stack = lax.psum(jnp.stack(partials), "freq")
    for level in range(len(masks)):
        migrated = migrated + masks[level] * summed_stack[level][None]
    return migrated


def solution(mesh):
    return jax.shard_map(
        local,
        mesh=mesh,
        in_specs=(
            P(("shot", "freq"), None, None, None),
            P("freq", None),
            P("freq", None, None),
            P("freq", None, None),
            P("shot"),
            P("shot"),
        ),
        out_specs=P(("shot", "freq"), None, None),
        check_vma=False,
    )
```

profile of v0, /device:TPU:0, one launch (start us, length us, event | category | flops | bytes accessed | tf_op | source)
XLA Modules:
  0.0 240.8 jit_solution(6213239613544791227)
XLA Ops:
  6.5 0.7 copy-done.3
  7.2 0.6 fusion.131
  9.7 1.7 select_bitcast_fusion
  11.5 0.3 slice_reduce_fusion.19
  11.8 0.6 fusion.130
  13.9 0.3 slice_reduce_fusion.13
  14.2 0.3 slice_reduce_fusion.7
  14.5 0.3 slice_reduce_fusion.1
  14.9 91.4 %all-reduce.30.cloned.1.call-done = (f32[32,1024]{1,0:T(8,128)}, f32[32,1024]{1,0:T(8,128)}, f32[32,1024]{1,0:T(8,128)}) async-done(((f32[32,1024]{1,0:T(8,128)}, f32[32,1024]{1,0:T(8,128)}, f32[32,1024]{1,0:T(8,128)}), (f32[32,1024]{1,0:T(8,128)}, f32[32,1024]{1,0:T(8,128)}, f32[32,1024]{1,0:T(8,128)})) %all-reduce.30.cloned.1.call-update) | async-done | bytes 393232 | tf_op jit(solution)/shard_map/psum | solution.py:15
  106.3 3.0 %multiply_subtract_fusion.71 = (f32[2,1,32,1024]{3,2,1,0:T(8,128)S(1)}, f32[2,1,32,1024]{3,2,1,0:T(8,128)S(1)}, f32[2,1,32,1024]{3,2,1,0:T(8,128)S(1)}, f32[2,1,...) fusion(f32[2]{0:T(128)S(1)} %get-tuple-element.29, ...), kind=kLoop, calls=%fused_computation.386 | loop fusion | flops 1900544 | bytes 2621496 | tf_op jit(solution)/shard_map/sub | solution.py:41
  109.4 0.3 select_maximum_fusion.4
  109.6 0.3 select_maximum_fusion.5
  110.0 0.6 slice_add_fusion.8
  110.6 0.6 slice_add_fusion.10
  111.3 0.2 multiply_subtract_fusion.69
  111.5 0.2 multiply_subtract_fusion.70
  111.8 0.6 fusion.10
  112.6 0.6 fusion.4
  113.2 0.2 multiply_subtract_fusion.68
  113.3 0.2 multiply_subtract_fusion.66
  113.5 0.2 multiply_subtract_fusion.67
  113.9 0.7 fusion.12
  114.7 0.7 fusion.6
  115.7 0.2 multiply_subtract_fusion.64
  116.1 0.7 fusion.14
  116.8 0.7 fusion.8
  117.5 0.2 multiply_subtract_fusion.62
  118.3 0.8 copy-done.2
  119.1 1.5 multiply_subtract_fusion.47
  120.6 0.3 select_maximum_fusion.2
  120.9 0.3 select_maximum_fusion.3
  121.3 0.6 slice_add_fusion.4
  121.9 0.6 slice_add_fusion.6
  122.5 0.2 multiply_subtract_fusion.45
  122.8 0.2 multiply_subtract_fusion.46
  123.1 0.6 fusion.22
  123.8 0.6 fusion.16
  124.8 0.2 multiply_subtract_fusion.43
  125.1 0.7 fusion.24
  125.9 0.7 fusion.18
  126.9 0.2 multiply_subtract_fusion.40
  127.3 0.7 fusion.26
  128.1 0.7 fusion.20
  129.1 0.2 multiply_subtract_fusion.37
  129.5 0.8 copy-done.1
  130.3 1.5 multiply_subtract_fusion.23
  131.9 0.3 select_maximum_fusion
  132.1 0.6 slice_add_fusion
  132.8 0.3 select_maximum_fusion.1
  133.0 0.6 slice_add_fusion.2
  133.7 0.2 multiply_subtract_fusion.22
  133.9 0.3 multiply_subtract_fusion.21
  134.3 0.6 fusion.34
  135.0 0.6 fusion.28
  136.0 0.2 multiply_subtract_fusion.19
  136.4 0.7 fusion.36
  137.1 0.7 fusion.30
  138.2 0.2 multiply_subtract_fusion.16
  138.5 0.7 fusion.38
  139.3 0.7 fusion.32
  140.3 0.2 multiply_subtract_fusion.13
  140.9 0.8 pad_maximum_fusion
  143.6 88.7 %all-reduce.28.cloned.1.call-done = f32[3,32,1024]{2,1,0:T(8,128)} async-done(((f32[3,32,1024]{2,1,0:T(8,128)}), f32[3,32,1024]{2,1,0:T(8,128)}) %all-reduce.28.cloned.1.call-update) | async-done | bytes 393232 | tf_op jit(solution)/shard_map/psum | solution.py:116
  232.3 1.7 fusion.112
  (79 shorter events, 6.2 us)
Async XLA Ops:
  6.5 99.8 %all-reduce.30.cloned.1.call-start = ((), (), s32[]{:S(2)}) async-start(), calls=%async_computation.1 | async-start | bytes 786432 | tf_op jit(solution)/shard_map/psum | solution.py:15
  6.5 0.7 copy-start.3
  9.7 1.8 copy-start.5
  9.7 2.1 copy-start.6
  9.7 4.0 %copy-start.4 = (f32[2,2]{1,0:T(2,128)S(1)}, f32[2,2]{1,0:T(2,128)}, u32[]{:S(2)}) copy-start(f32[2,2]{1,0:T(2,128)} %param.7) | copy-start | bytes 52
  11.4 95.0 %copy-start = (f32[2,2,32,1024]{3,2,1,0:T(8,128)S(1)}, f32[2,2,32,1024]{3,2,1,0:T(8,128)}, u32[]{:S(2)}) copy-start(f32[2,2,32,1024]{3,2,1,0:T(8,128)} %param.6) | copy-start | bytes 1572868
  11.4 220.9 %all-reduce.28.cloned.1.call-start = ((), (), s32[]{:S(2)}) async-start(), calls=%async_computation | async-start | bytes 786432 | tf_op jit(solution)/shard_map/psum | solution.py:116
  118.2 0.9 copy-start.2
  129.4 0.9 copy-start.1
Sparse Core Ops, SparseCore 0:
  11.5 94.7 all-reduce.29
  141.9 90.3 all-reduce.27
where the time goes:
time: 241 us
  waiting for transfers between devices  180 us (75%)
  other arithmetic  36.8 us (15%)
  between operations  19.1 us (8%)
  local copies, waits for them, and re-layouts  4.73 us (2%)
    psum x1, waiting for transfers between devices, broadcast(): return lax.psum(kept, axis)  91.4 us
    psum x1, waiting for transfers between devices, local(): summed_stack = lax.psum(jnp.stack(partials), 'freq')  88.7 us
    add x24, other arithmetic, directional(): outer_pair = adjacent(2) + adjacent(-2)  15.3 us
    sub x36, other arithmetic, complex_mul(): values[:, 0] * coef_re - values[:, 1] * coef_im  12.8 us
  transfers between devices with their start and end apart: 2, of which 2 were waited for; matrix products, arithmetic and copies ran while one was open for 1% of the time, Pallas kernels for 0%

commit v1 on v0

v1 whole, which is shorter than its diff:
```python
import functools
import math

import jax
import jax.numpy as jnp
from jax import lax
from jax.experimental import pallas as pl
from jax.experimental.pallas import tpu as pltpu
from jax.sharding import PartitionSpec as P

lens_rate = 3.0
wave_rate = 0.5
MESH = pl.DeviceIdType.MESH
SUB = 8
LANE = 128
TOP = 8


def sincos(x):
    k = jnp.floor(x * (2.0 / math.pi) + 0.5)
    r = x - k * 1.5703125
    r = r - k * 4.837512969970703125e-4
    r = r - k * 7.54978995489188216e-8
    q = k.astype(jnp.int32)
    z = r * r
    s = r + r * z * (-1.6666654611e-1 + z * (8.3321608736e-3 - z * 1.9515295891e-4))
    c = 1.0 - 0.5 * z + z * z * (
        4.166664568298827e-2 + z * (-1.388731625493765e-3 + z * 2.443315711809948e-5)
    )
    swap = (q & 1) == 1
    sin = jnp.where(swap, c, s)
    cos = jnp.where(swap, s, c)
    sin = jnp.where((q & 2) == 2, -sin, sin)
    cos = jnp.where(((q + 1) & 2) == 2, -cos, cos)
    return sin, cos


def kernel(
    n,
    owner,
    position,
    spectrum,
    taps,
    recv_hbm,
    slow,
    out,
    rbuf,
    fx,
    fy,
    all_slow,
    picked,
    slabs,
    parts,
    red,
    image,
    load_sem,
    a_send,
    a_recv,
    b_send,
    b_recv,
    c_send,
    c_recv,
    d_send,
    d_recv,
):
    me = lax.axis_index("freq")
    steps = owner.shape[0]
    fl = rbuf.shape[0]
    height = rbuf.shape[2]
    breadth = rbuf.shape[3]
    nb = breadth // LANE
    nrt = height // SUB
    cr = slow.shape[1]
    freq_total = n * fl
    first = me * fl

    def peer(i):
        return lax.rem(me + i, n)

    def remote(src, dst, send, recv, to):
        return pltpu.make_async_remote_copy(
            src_ref=src, dst_ref=dst, send_sem=send, recv_sem=recv,
            device_id={"freq": to}, device_id_type=MESH,
        )

    load = pltpu.make_async_copy(recv_hbm, rbuf, load_sem)
    load.start()
    barrier = pltpu.get_barrier_semaphore()
    for i in range(1, n):
        pl.semaphore_signal(barrier, inc=1, device_id={"freq": peer(i)}, device_id_type=MESH)
    pl.semaphore_wait(barrier, n - 1)

    a_copies = [
        remote(slow.at[peer(i)], all_slow.at[me], a_send.at[i], a_recv.at[i], peer(i))
        for i in range(1, n)
    ]
    for copy in a_copies:
        copy.start()
    all_slow[me] = slow[me]

    def pieces(rt, cb):
        row = (rt * nb + cb) * SUB
        size = min(cr, SUB)
        return [((row + o) // cr, (row + o) % cr, size, o) for o in range(0, SUB, size)]

    def tile_load(ref, rt, cb):
        got = [ref[c, r : r + m] for c, r, m, _ in pieces(rt, cb)]
        return got[0] if len(got) == 1 else jnp.concatenate(got, axis=0)

    def tile_store(ref, rt, cb, value):
        for c, r, m, o in pieces(rt, cb):
            ref[c, r : r + m] = value[o : o + m]

    def rows(rt, k=0):
        start = TOP + rt * SUB + k
        return slice(start, start + SUB)

    lanes = lax.broadcasted_iota(jnp.int32, (SUB, LANE), 1)
    subs = lax.broadcasted_iota(jnp.int32, (SUB, LANE), 0)
    zero = jnp.zeros((SUB, LANE), jnp.float32)

    @pl.loop(0, fl * 2)
    def _(field):
        for part in range(2):
            for cb in range(nb):
                for buf in (fx, fy):
                    buf[field, part, cb, 0:TOP] = zero
                    buf[field, part, cb, TOP + height : 2 * TOP + height] = zero

    src_row = position[0].astype(jnp.float32)
    src_col = position[1].astype(jnp.float32)
    for rt in range(nrt):
        for cb in range(nb):
            row = (subs + rt * SUB).astype(jnp.float32) - src_row
            col = (lanes + cb * LANE).astype(jnp.float32) - src_col
            distance = jnp.sqrt(row * row + col * col + 1.0)
            amplitude = 1.0 / (1.0 + distance / (height / 4.0))
            for f in range(fl):
                number = ((first + f).astype(jnp.float32) + 1.0) * (wave_rate / freq_total)
                sin, cos = sincos(number * distance)
                base_re = amplitude * cos
                base_im = -amplitude * sin
                wr = spectrum[f, 0]
                wi = spectrum[f, 1]
                fx[2 * f, 0, cb, rows(rt)] = wr * base_re - wi * base_im
                fx[2 * f, 1, cb, rows(rt)] = wr * base_im + wi * base_re
    load.wait()
    for f in range(fl):
        for rt in range(nrt):
            for cb in range(nb):
                at = (slice(rt * SUB, rt * SUB + SUB), slice(cb * LANE, cb * LANE + LANE))
                fx[2 * f + 1, 0, cb, rows(rt)] = rbuf[(f, 0) + at]
                fx[2 * f + 1, 1, cb, rows(rt)] = -rbuf[(f, 1) + at]

    for copy in a_copies:
        copy.wait_recv()
    b_copies = []
    for t in range(steps):
        picked[t] = all_slow[owner[t]]
        slabs[t, me] = picked[t]
        sends = [
            remote(picked.at[t], slabs.at[t, me], b_send.at[t, i], b_recv.at[t, i], peer(i))
            for i in range(1, n)
        ]
        for copy in sends:
            copy.start()
        b_copies.append(sends)

    def column_shift(get, s):
        memo = {}

        def rolled(cb):
            if cb < 0 or cb >= nb:
                return zero
            if cb not in memo:
                memo[cb] = pltpu.roll(get(cb), (-s) % LANE, 1)
            return memo[cb]

        def at(cb):
            if s > 0:
                return jnp.where(lanes >= LANE - s, rolled(cb + 1), rolled(cb))
            return jnp.where(lanes < -s, rolled(cb - 1), rolled(cb))

        return at

    def combine(c, x, one, two):
        (xr, xi), (pr, pi), (qr, qi) = x, one, two
        re = (c[0] * xr - c[1] * xi) + (c[2] * pr - c[3] * pi) + (c[4] * qr - c[5] * qi)
        im = (c[0] * xi + c[1] * xr) + (c[2] * pi + c[3] * pr) + (c[4] * qi + c[5] * qr)
        return re, im

    def coefficients(f, d):
        return [taps[f, d, j] for j in range(6)]

    def lens(buf, slab):
        @pl.loop(0, fl)
        def _(f):
            rate = ((first + f).astype(jnp.float32) + 1.0) * (lens_rate / freq_total)
            for rt in range(nrt):
                for cb in range(nb):
                    sin, cos = sincos(rate * tile_load(slab, rt, cb))
                    for s in range(2):
                        re = buf[2 * f + s, 0, cb, rows(rt)]
                        im = buf[2 * f + s, 1, cb, rows(rt)]
                        buf[2 * f + s, 0, cb, rows(rt)] = re * cos + im * sin
                        buf[2 * f + s, 1, cb, rows(rt)] = im * cos - re * sin

    def rows_then_columns(src, dst):
        @pl.loop(0, fl * 2)
        def _(field):
            f = lax.div(field, 2)
            c0 = coefficients(f, 0)
            c1 = coefficients(f, 1)
            for rt in range(nrt):
                memo = {}

                def down(cb):
                    if cb not in memo:
                        x = [src[field, p, cb, rows(rt)] for p in range(2)]
                        one = [src[field, p, cb, rows(rt, 1)] + src[field, p, cb, rows(rt, -1)] for p in range(2)]
                        two = [src[field, p, cb, rows(rt, 2)] + src[field, p, cb, rows(rt, -2)] for p in range(2)]
                        memo[cb] = combine(c0, x, one, two)
                    return memo[cb]

                moved = [
                    {s: column_shift(lambda cb, p=p: down(cb)[p], s) for s in (1, -1, 2, -2)}
                    for p in range(2)
                ]
                for cb in range(nb):
                    one = [moved[p][1](cb) + moved[p][-1](cb) for p in range(2)]
                    two = [moved[p][2](cb) + moved[p][-2](cb) for p in range(2)]
                    re, im = combine(c1, down(cb), one, two)
                    dst[field, 0, cb, rows(rt)] = re
                    dst[field, 1, cb, rows(rt)] = im

    def slanted(src, field, c, rt, side):
        moved = [
            {
                s: column_shift(lambda cb, p=p, s=s: src[field, p, cb, rows(rt, s)], s * side)
                for s in (1, -1, 2, -2)
            }
            for p in range(2)
        ]

        def at(cb):
            x = [src[field, p, cb, rows(rt)] for p in range(2)]
            one = [moved[p][1](cb) + moved[p][-1](cb) for p in range(2)]
            two = [moved[p][2](cb) + moved[p][-2](cb) for p in range(2)]
            return combine(c, x, one, two)

        return at

    def first_slant(src, dst):
        @pl.loop(0, fl * 2)
        def _(field):
            c = coefficients(lax.div(field, 2), 2)
            for rt in range(nrt):
                at = slanted(src, field, c, rt, 1)
                for cb in range(nb):
                    re, im = at(cb)
                    dst[field, 0, cb, rows(rt)] = re
                    dst[field, 1, cb, rows(rt)] = im

    def second_slant(src, dst, part, keep):
        for f in range(fl):
            c = coefficients(f, 3)
            for rt in range(nrt):
                source = slanted(src, 2 * f, c, rt, -1)
                receiver = slanted(src, 2 * f + 1, c, rt, -1)
                for cb in range(nb):
                    sr, si = source(cb)
                    rr, ri = receiver(cb)
                    if keep:
                        dst[2 * f, 0, cb, rows(rt)] = sr
                        dst[2 * f, 1, cb, rows(rt)] = si
                        dst[2 * f + 1, 0, cb, rows(rt)] = rr
                        dst[2 * f + 1, 1, cb, rows(rt)] = ri
                    term = sr * rr - si * ri
                    if f > 0:
                        term = tile_load(part, rt, cb) + term
                    tile_store(part, rt, cb, term)

    now, later = fx, fy
    c_copies = []
    for t in range(steps):
        for copy in b_copies[t]:
            copy.wait_recv()
        lens(now, slabs.at[t])
        rows_then_columns(now, later)
        first_slant(later, now)
        second_slant(now, later, parts.at[t], t < steps - 1)
        now, later = later, now
        sends = [
            remote(parts.at[t, peer(i)], red.at[t, me], c_send.at[t, i], c_recv.at[t, i], peer(i))
            for i in range(1, n)
        ]
        for copy in sends:
            copy.start()
        red[t, me] = parts[t, me]
        c_copies.append(sends)

    sums = []
    for t in range(steps):
        for copy in c_copies[t]:
            copy.wait_recv()
        total = red[t, 0]
        for i in range(1, n):
            total = total + red[t, i]
        sums.append(total / math.sqrt(freq_total))
    for k in range(n):
        value = sums[0] * (owner[0] == k).astype(jnp.float32)
        for t in range(1, steps):
            value = value + sums[t] * (owner[t] == k).astype(jnp.float32)
        image[k] = value
    d_copies = [
        remote(image.at[peer(i)], out.at[me], d_send.at[i], d_recv.at[i], peer(i))
        for i in range(1, n)
    ]
    for copy in d_copies:
        copy.start()
    out[me] = image[me]
    for copy in d_copies:
        copy.wait_recv()
    for copy in a_copies + sum(b_copies, []) + sum(c_copies, []) + d_copies:
        copy.wait_send()


def local(n, receiver_data, source_spectrum, filter_taps, slowness, depth_owner, source_position):
    fl, _, height, breadth = receiver_data.shape
    steps = depth_owner.shape[0]
    nb = breadth // LANE
    nrt = height // SUB
    cr = height * nb // n
    slab = slowness[0].reshape(nrt, SUB, nb, LANE).transpose(0, 2, 1, 3).reshape(n, cr, LANE)
    chunks = (n, cr, LANE)
    smem = pl.BlockSpec(memory_space=pltpu.SMEM)
    vmem = pl.BlockSpec(memory_space=pltpu.VMEM)
    fields = (2 * fl, 2, nb, height + 2 * TOP, LANE)
    dma = pltpu.SemaphoreType.DMA
    result = pl.pallas_call(
        functools.partial(kernel, n),
        out_shape=jax.ShapeDtypeStruct(chunks, jnp.float32),
        in_specs=[smem, smem, smem, smem, pl.BlockSpec(memory_space=pl.ANY), vmem],
        out_specs=vmem,
        scratch_shapes=[
            pltpu.VMEM(receiver_data.shape, jnp.float32),
            pltpu.VMEM(fields, jnp.float32),
            pltpu.VMEM(fields, jnp.float32),
            pltpu.VMEM(chunks, jnp.float32),
            pltpu.VMEM((steps, cr, LANE), jnp.float32),
            pltpu.VMEM((steps,) + chunks, jnp.float32),
            pltpu.VMEM((steps,) + chunks, jnp.float32),
            pltpu.VMEM((steps,) + chunks, jnp.float32),
            pltpu.VMEM(chunks, jnp.float32),
            dma,
            dma((n,)),
            dma((n,)),
            dma((steps, n)),
            dma((steps, n)),
            dma((steps, n)),
            dma((steps, n)),
            dma((n,)),
            dma((n,)),
        ],
        compiler_params=pltpu.CompilerParams(
            collective_id=0, has_side_effects=True, vmem_limit_bytes=48 * 1024 * 1024
        ),
        name="migrate",
    )(depth_owner, source_position, source_spectrum, filter_taps, receiver_data, slab)
    image = result.reshape(nrt, nb, SUB, LANE).transpose(0, 2, 1, 3)
    return image.reshape(1, height, breadth)


def solution(mesh):
    return jax.shard_map(
        functools.partial(local, mesh.shape["freq"]),
        mesh=mesh,
        in_specs=(
            P(("shot", "freq"), None, None, None),
            P("freq", None),
            P("freq", None, None),
            P("freq", None, None),
            P("shot"),
            P("shot"),
        ),
        out_specs=P(("shot", "freq"), None, None),
        check_vma=False,
    )
```

time: 241 us -> 47.6 us (0.20)
  waiting for transfers between devices: 180 us -> 0 us
  Pallas kernels: 0 us -> 42.7 us
  other arithmetic: 36.8 us -> 0 us
  between operations: 19.1 us -> 0.02 us
    psum x2 -> x0, waiting for transfers between devices: 180 us -> none  [the longest x1 91.4 us: broadcast(): return lax.psum(kept, axis)]
    pallas_call x0 -> x1, Pallas kernels: none -> 42.7 us  [local(): pl.pallas_call(functools.partial(kernel, n), out_shape=jax.ShapeDtypeStru...]
    add x51 -> x0, other arithmetic: 19.7 us -> none  [the longest x24 15.3 us: directional(): outer_pair = adjacent(2) + adjacent(-2)]
    sub x36 -> x0, other arithmetic: 12.8 us -> none  [complex_mul(): values[:, 0] * coef_re - values[:, 1] * coef_im]
    slice x8 -> x0, local copies, waits for them, and re-layouts: 2.48 us -> none  [the longest x4 1.02 us: directional(): return result + complex_mul(outer_pair, coeffs[:, 4], handed * coeffs[:, 5])]
  transfers between devices with their start and end apart: 2 -> 0, of which waited for: 2 -> 0; matrix products, arithmetic and copies ran while one was open for 1% -> 0% of each run, Pallas kernels for 0% -> 0%
where the time goes in v1:
time: 47.6 us; the launch traced here: 47.3 us
  Pallas kernels  42.7 us (90%)
  local copies, waits for them, and re-layouts  4.64 us (10%)
    pallas_call x1, Pallas kernels, local(): pl.pallas_call(functools.partial(kernel, n), out_shape=jax.ShapeDtypeStru...  42.7 us
    unnamed x13, local copies, waits for them, and re-layouts  4.64 us

profile of v1, /device:TPU:0, one launch (start us, length us, event | category | flops | bytes accessed | tf_op | source)
XLA Modules:
  0.0 47.3 jit_solution(7629911456058970367)
XLA Ops:
  0.0 0.0 copy-start.4
  0.0 0.0 copy-start.3
  0.0 0.7 %copy-done.4 = s32[3]{0:T(128)S(1)} copy-done((s32[3]{0:T(128)S(1)}, s32[3]{0:T(128)}, u32[]{:S(2)}) %copy-start.4) | copy-done | bytes 36
  0.7 0.0 copy-done.3
  0.7 0.0 copy-start
  0.7 1.0 %copy-done = f32[2,2,32,1024]{3,2,1,0:T(8,128)S(1)} copy-done((f32[2,2,32,1024]{3,2,1,0:T(8,128)S(1)}, f32[2,2,32,1024]{3,2,1,0:T(8,128)}, u32[]{:S(2)}) %copy-start) | copy-done | bytes 524312
  1.7 0.0 copy-start.1
  1.7 0.9 %copy-done.1 = f32[1,32,1024]{2,1,0:T(8,128)S(1)} copy-done((f32[1,32,1024]{2,1,0:T(8,128)S(1)}, f32[1,32,1024]{2,1,0:T(8,128)}, u32[]{:S(2)}) %copy-start.1) | copy-done | bytes 131096
  2.6 0.0 copy-start.2
  2.6 0.7 %copy-done.2 = f32[2,4,6]{2,1,0:T(4,128)S(1)} copy-done((f32[2,4,6]{2,1,0:T(4,128)S(1)}, f32[2,4,6]{2,1,0:T(4,128)}, u32[]{:S(2)}) %copy-start.2) | copy-done | bytes 216
  3.3 0.0 copy-start.5
  3.3 0.7 %copy-done.5 = s32[2]{0:T(128)S(1)} copy-done((s32[2]{0:T(128)S(1)}, s32[2]{0:T(128)}, u32[]{:S(2)}) %copy-start.5) | copy-done | bytes 32
  4.0 42.7 %migrate.1 = f32[16,16,128]{2,1,0:T(8,128)S(1)} custom-call(s32[3]{0:T(128)S(1)} %copy-done.4, s32[2]{0:T(128)S(1)} %copy-done.5, f32[2,2]{1,0:T(2,128)S(1)} %copy-done.3, f32[2,4,6]{2,1,0:T(4,128)S(1)} %copy-done.2, f32[2,2,32,1024]{3,2,1,0:T(8,128)S(1)} %copy-done, f32[16,16,128]{2,1,0:T(8,128)S(1)} %bitcast.11), custom_call_target="tpu_custom_call" | custom-call | tf_op jit(solution)/shard_map/migrate/pallas_call | solution.py:340
  46.7 0.7 %copy.8 = f32[1,32,1024]{2,1,0:T(8,128)} copy(f32[1,32,1024]{2,1,0:T(8,128)S(1)} %bitcast.10) | data formatting | bytes 262144
Async XLA Ops:
  0.0 0.7 %copy-start.4 = (s32[3]{0:T(128)S(1)}, s32[3]{0:T(128)}, u32[]{:S(2)}) copy-start(s32[3]{0:T(128)} %owner.1) | copy-start | bytes 40
  0.0 0.7 %copy-start.3 = (f32[2,2]{1,0:T(2,128)S(1)}, f32[2,2]{1,0:T(2,128)}, u32[]{:S(2)}) copy-start(f32[2,2]{1,0:T(2,128)} %spectrum.1) | copy-start | bytes 52
  0.7 1.0 %copy-start = (f32[2,2,32,1024]{3,2,1,0:T(8,128)S(1)}, f32[2,2,32,1024]{3,2,1,0:T(8,128)}, u32[]{:S(2)}) copy-start(f32[2,2,32,1024]{3,2,1,0:T(8,128)} %recv_hbm.1) | copy-start | bytes 1572868
  1.7 0.9 %copy-start.1 = (f32[1,32,1024]{2,1,0:T(8,128)S(1)}, f32[1,32,1024]{2,1,0:T(8,128)}, u32[]{:S(2)}) copy-start(f32[1,32,1024]{2,1,0:T(8,128)} %param.9) | copy-start | bytes 393220
  2.6 0.7 %copy-start.2 = (f32[2,4,6]{2,1,0:T(4,128)S(1)}, f32[2,4,6]{2,1,0:T(4,128)}, u32[]{:S(2)}) copy-start(f32[2,4,6]{2,1,0:T(4,128)} %taps.1) | copy-start | bytes 580
  3.3 0.7 %copy-start.5 = (s32[2]{0:T(128)S(1)}, s32[2]{0:T(128)}, u32[]{:S(2)}) copy-start(s32[2]{0:T(128)} %position.1) | copy-start | bytes 28

commit v2 on v1

--- a/solution.py
+++ b/solution.py
@@ -54,6 +54,7 @@
     red,
     image,
     load_sem,
+    own_sem,
     a_send,
     a_recv,
     b_send,
@@ -75,7 +76,16 @@
     first = me * fl
 
     def peer(i):
-        return lax.rem(me + i, n)
+        if n & (n - 1):
+            return lax.rem(me + i, n)
+        to = 0
+        for b in range(n.bit_length() - 1):
+            bit = lax.rem(lax.div(me, 1 << b), 2)
+            to = to + (1 << b) * (1 - bit if i >> b & 1 else bit)
+        return to
+
+    partners = [peer(i) for i in range(n)]
+    rounds = range(n - 1, 0, -1)
 
     def remote(src, dst, send, recv, to):
         return pltpu.make_async_remote_copy(
@@ -86,17 +96,18 @@
     load = pltpu.make_async_copy(recv_hbm, rbuf, load_sem)
     load.start()
     barrier = pltpu.get_barrier_semaphore()
-    for i in range(1, n):
-        pl.semaphore_signal(barrier, inc=1, device_id={"freq": peer(i)}, device_id_type=MESH)
+    for i in rounds:
+        pl.semaphore_signal(barrier, inc=1, device_id={"freq": partners[i]}, device_id_type=MESH)
     pl.semaphore_wait(barrier, n - 1)
 
     a_copies = [
-        remote(slow.at[peer(i)], all_slow.at[me], a_send.at[i], a_recv.at[i], peer(i))
-        for i in range(1, n)
+        remote(slow.at[partners[i]], all_slow.at[me], a_send.at[i], a_recv.at[i], partners[i])
+        for i in rounds
     ]
     for copy in a_copies:
         copy.start()
-    all_slow[me] = slow[me]
+    own = pltpu.make_async_copy(slow.at[me], all_slow.at[me], own_sem)
+    own.start()
 
     def pieces(rt, cb):
         row = (rt * nb + cb) * SUB
@@ -152,19 +163,32 @@
                 fx[2 * f + 1, 0, cb, rows(rt)] = rbuf[(f, 0) + at]
                 fx[2 * f + 1, 1, cb, rows(rt)] = -rbuf[(f, 1) + at]
 
+    own.wait()
     for copy in a_copies:
         copy.wait_recv()
     b_copies = []
     for t in range(steps):
-        picked[t] = all_slow[owner[t]]
-        slabs[t, me] = picked[t]
+        value = all_slow[owner[t]]
+        picked[t] = value
+        slabs[t, me] = value
         sends = [
-            remote(picked.at[t], slabs.at[t, me], b_send.at[t, i], b_recv.at[t, i], peer(i))
-            for i in range(1, n)
+            remote(picked.at[t], slabs.at[t, me], b_send.at[t, i], b_recv.at[t, i], partners[i])
+            for i in rounds
         ]
-        for copy in sends:
+        b_copies.append(sends)
+
+    def begin(copies):
+        for copy in copies:
             copy.start()
-        b_copies.append(sends)
+
+    def left(copies):
+        for copy in copies:
+            copy.wait_send()
+
+    begin(b_copies[0])
+    left(b_copies[0])
+    if steps > 1:
+        begin(b_copies[1])
 
     def column_shift(get, s):
         memo = {}
@@ -262,9 +286,9 @@
                     dst[field, 1, cb, rows(rt)] = im
 
     def second_slant(src, dst, part, keep):
-        for f in range(fl):
-            c = coefficients(f, 3)
-            for rt in range(nrt):
+        for rt in range(nrt):
+            for f in range(fl):
+                c = coefficients(f, 3)
                 source = slanted(src, 2 * f, c, rt, -1)
                 receiver = slanted(src, 2 * f + 1, c, rt, -1)
                 for cb in range(nb):
@@ -285,14 +309,17 @@
     for t in range(steps):
         for copy in b_copies[t]:
             copy.wait_recv()
+        if 0 < t < steps - 1:
+            left(b_copies[t])
+            begin(b_copies[t + 1])
         lens(now, slabs.at[t])
         rows_then_columns(now, later)
         first_slant(later, now)
         second_slant(now, later, parts.at[t], t < steps - 1)
         now, later = later, now
         sends = [
-            remote(parts.at[t, peer(i)], red.at[t, me], c_send.at[t, i], c_recv.at[t, i], peer(i))
-            for i in range(1, n)
+            remote(parts.at[t, partners[i]], red.at[t, me], c_send.at[t, i], c_recv.at[t, i], partners[i])
+            for i in rounds
         ]
         for copy in sends:
             copy.start()
@@ -313,15 +340,15 @@
             value = value + sums[t] * (owner[t] == k).astype(jnp.float32)
         image[k] = value
     d_copies = [
-        remote(image.at[peer(i)], out.at[me], d_send.at[i], d_recv.at[i], peer(i))
-        for i in range(1, n)
+        remote(image.at[partners[i]], out.at[me], d_send.at[i], d_recv.at[i], partners[i])
+        for i in rounds
     ]
     for copy in d_copies:
         copy.start()
     out[me] = image[me]
     for copy in d_copies:
         copy.wait_recv()
-    for copy in a_copies + sum(b_copies, []) + sum(c_copies, []) + d_copies:
+    for copy in a_copies + b_copies[-1] * (steps > 1) + sum(c_copies, []) + d_copies:
         copy.wait_send()
 
 
@@ -335,12 +362,13 @@
     chunks = (n, cr, LANE)
     smem = pl.BlockSpec(memory_space=pltpu.SMEM)
     vmem = pl.BlockSpec(memory_space=pltpu.VMEM)
+    hbm = pl.BlockSpec(memory_space=pltpu.HBM)
     fields = (2 * fl, 2, nb, height + 2 * TOP, LANE)
     dma = pltpu.SemaphoreType.DMA
     result = pl.pallas_call(
         functools.partial(kernel, n),
         out_shape=jax.ShapeDtypeStruct(chunks, jnp.float32),
-        in_specs=[smem, smem, smem, smem, pl.BlockSpec(memory_space=pl.ANY), vmem],
+        in_specs=[smem, smem, smem, smem, hbm, hbm],
         out_specs=vmem,
         scratch_shapes=[
             pltpu.VMEM(receiver_data.shape, jnp.float32),
@@ -353,6 +381,7 @@
             pltpu.VMEM((steps,) + chunks, jnp.float32),
             pltpu.VMEM(chunks, jnp.float32),
             dma,
+            dma,
             dma((n,)),
             dma((n,)),
             dma((steps, n)),
@@ -363,7 +392,7 @@
             dma((n,)),
         ],
         compiler_params=pltpu.CompilerParams(
-            collective_id=0, has_side_effects=True, vmem_limit_bytes=48 * 1024 * 1024
+            collective_id=0, has_side_effects=True, vmem_limit_bytes=60 * 1024 * 1024
         ),
         name="migrate",
     )(depth_owner, source_position, source_spectrum, filter_taps, receiver_data, slab)

time: 47.6 us -> 48.3 us (1.015)
  Pallas kernels: 42.7 us -> 46.4 us
  local copies, waits for them, and re-layouts: 4.64 us -> 1.57 us
    pallas_call x1, Pallas kernels: 42.7 us -> 46.4 us  [local(): pl.pallas_call(functools.partial(kernel, n), out_shape=jax.ShapeDtypeStru...]
    unnamed x13 -> x1, local copies, waits for them, and re-layouts: 4.64 us -> 1.57 us
where the time goes in v2:
time: 48.3 us; the launch traced here: 48 us
  Pallas kernels  46.4 us (96%)
  local copies, waits for them, and re-layouts  1.57 us (3%)
    pallas_call x1, Pallas kernels, local(): pl.pallas_call(functools.partial(kernel, n), out_shape=jax.ShapeDtypeStru...  46.4 us
    unnamed x1, local copies, waits for them, and re-layouts  1.57 us

profile of v2, /device:TPU:0, one launch (start us, length us, event | category | flops | bytes accessed | tf_op | source)
XLA Modules:
  0.0 48.0 jit_solution(16854741678495345243)
XLA Ops:
  0.0 46.4 %migrate.1 = f32[16,16,128]{2,1,0:T(8,128)} custom-call(s32[3]{0:T(128)} %owner.1, s32[2]{0:T(128)} %position.1, f32[2,2]{1,0:T(2,128)} %spectrum.1, f32[2,4,6]{2,1,0:T(4,128)} %taps.1, f32[2,2,32,1024]{3,2,1,0:T(8,128)} %recv_hbm.1, f32[16,16,128]{2,1,0:T(8,128)} %bitcast.11), custom_call_target="tpu_custom_call" | custom-call | tf_op jit(solution)/shard_map/migrate/pallas_call | solution.py:368
  46.4 1.6 %copy.8 = f32[1,32,1024]{2,1,0:T(8,128)} copy(f32[1,32,1024]{2,1,0:T(8,128)} %bitcast.10) | data formatting | bytes 262144
